TPU v7x, 32 devices: a whole 2x2x4 slice. The times are simulated.
32 devices in a mesh: seq: 4 (over x, core), clip: 8 (over z, y).
Axes of the slice: x: 2, y: 2, z: 4, core: 2. Of those that a mesh axis runs over, the one named last changes fastest.
Arguments:
- x_vis: bfloat16 [24, 157, 768], P('clip'), may hold values from -6 to 6
- vis_pos: int32 [24, 157], P('clip'), may hold values from 0 to 1567, as said below
- w_proj: bfloat16 [768, 384], replicated, may hold values from -0.21875 to 0.21875
- b_proj: float32 [384], replicated, may hold values from -3 to 3
- mask_token: float32 [384], replicated, may hold values from -4 to 4
- ln1_gain: float32 [384], replicated, may hold values from 0.25 to 1.75
- ln1_bias: float32 [384], replicated, may hold values from -2 to 2
- w_qkv: bfloat16 [384, 1152], replicated, may hold values from -0.3125 to 0.3125
- q_bias: float32 [384], replicated, may hold values from -2 to 2
- v_bias: float32 [384], replicated, may hold values from -3 to 3
- w_out: bfloat16 [384, 384], replicated, may hold values from -4 to 4
- b_out: float32 [384], replicated, may hold values from -2 to 2
- ln2_gain: float32 [384], replicated, may hold values from 0.25 to 1.75
- ln2_bias: float32 [384], replicated, may hold values from -2 to 2
- w_fc1: bfloat16 [384, 1536], replicated, may hold values from -0.3125 to 0.3125
- b_fc1: float32 [1536], replicated, may hold values from -3 to 3
- w_fc2: bfloat16 [1536, 384], replicated, may hold values from -0.15625 to 0.15625
- b_fc2: float32 [384], replicated, may hold values from -2 to 2
- cotangent: bfloat16 [24, 1568, 384], P('clip', 'seq'), may hold values from -6 to 6
Outputs:
- output: bfloat16 [24, 1568, 384], P('clip', 'seq')
- grad_x: float32 [24, 157, 768], P('clip')
- grad_w_proj: float32 [768, 384], replicated
- grad_b_proj: float32 [384], replicated
- grad_mask: float32 [384], replicated
- grad_ln1_gain: float32 [384], replicated
- grad_ln1_bias: float32 [384], replicated
- grad_w_qkv: float32 [384, 1152], replicated
- grad_q_bias: float32 [384], replicated
- grad_v_bias: float32 [384], replicated
- grad_w_out: float32 [384, 384], replicated
- grad_b_out: float32 [384], replicated
- grad_ln2_gain: float32 [384], replicated
- grad_ln2_bias: float32 [384], replicated
- grad_w_fc1: float32 [384, 1536], replicated
- grad_b_fc1: float32 [1536], replicated
- grad_w_fc2: float32 [1536, 384], replicated
- grad_b_fc2: float32 [384], replicated
- trust: float32 [4], replicated
- trust_qkv: float32 [1], replicated
Inputs may be any that keep to these rules, and one draw needn't show every extreme that they name: `vis_pos`: each clip's 157 visible positions, in rising order, all different.
All inputs are finite; a program needn't handle non-finite values.
Results may differ from a plain program's by a relative error of at most 0.01.
Values may be sent and summed in bfloat16 or wider, within the bound.
No kernel may reach another device: no remote copies, remote signals or barrier semaphores. Data moves between devices by JAX's collectives and lax.ppermute only.
A program may use at most 256 MiB of HBM per device.

v0:
```python
import math
import jax
import jax.numpy as jnp
from jax import lax
from jax.sharding import PartitionSpec as P

D = 384
HEADS = 6
HEAD = 64
LEN = 1568
exact_prec = lax.Precision.HIGHEST


def sinusoid(length, columns):
    positions = jnp.arange(length, dtype=jnp.float32)[:, None]
    column = jnp.arange(columns, dtype=jnp.int32)
    exponent = (2 * (column // 2)).astype(jnp.float32) / columns
    angles = positions / jnp.power(10000.0, exponent)[None, :]
    return jnp.where((column % 2)[None, :] == 0, jnp.sin(angles), jnp.cos(angles))


def layer_norm(inputs, gain_vec, shift_vec):
    average = jnp.mean(inputs, axis=-1, keepdims=True)
    centered = inputs - average
    variance = jnp.mean(centered * centered, axis=-1, keepdims=True)
    return centered * lax.rsqrt(variance + 1e-05) * gain_vec + shift_vec


def gelu_exact(values):
    return jax.nn.gelu(values, approximate=False)


def shards(
    x_vis,
    vis_pos,
    w_proj,
    b_proj,
    mask_token,
    ln1_gain,
    ln1_bias,
    w_qkv,
    q_bias,
    v_bias,
    w_out,
    b_out,
    ln2_gain,
    ln2_bias,
    w_fc1,
    b_fc1,
    w_fc2,
    b_fc2,
    cotangent,
):
    row_count = LEN // lax.axis_size("seq")
    score_scale = HEAD ** (-0.5)
    first_row = lax.axis_index("seq") * row_count
    projected = (
        jnp.einsum("cvi,id->cvd", x_vis, w_proj, preferred_element_type=jnp.float32) + b_proj
    )
    places = first_row + lax.iota(jnp.int32, row_count)
    onehot = (vis_pos[:, None, :] == places[None, :, None]).astype(jnp.float32)
    visible = jnp.sum(onehot, axis=2, keepdims=True)
    position_table = lax.dynamic_slice_in_dim(sinusoid(LEN, D), first_row, row_count, 0)
    embedded = (
        jnp.einsum("crv,cvd->crd", onehot, projected, precision=exact_prec)
        + (1.0 - visible) * mask_token
        + position_table
    )
    normed = layer_norm(embedded, ln1_gain, ln1_bias).astype(jnp.bfloat16)
    qkv_mixed = jnp.einsum("crd,de->cre", normed, w_qkv, preferred_element_type=jnp.float32)
    queries = (qkv_mixed[..., :D] + q_bias).astype(jnp.bfloat16)
    keys_local = qkv_mixed[..., D : 2 * D].astype(jnp.bfloat16)
    values_local = (qkv_mixed[..., 2 * D :] + v_bias).astype(jnp.bfloat16)
    keys_all, values_all = (
        lax.all_gather(keys_local, "seq", axis=1, tiled=True),
        lax.all_gather(values_local, "seq", axis=1, tiled=True),
    )

    def attend(sliced):
        query_one, key_one, value_one = sliced
        q_heads = query_one.reshape(row_count, HEADS, HEAD)
        k_heads = key_one.reshape(LEN, HEADS, HEAD)
        v_heads = value_one.reshape(LEN, HEADS, HEAD)
        scores = (
            jnp.einsum("qhe,khe->hqk", q_heads, k_heads, preferred_element_type=jnp.float32)
            * score_scale
        )
        largest = jnp.max(scores, axis=-1, keepdims=True)
        exponent = jnp.exp(scores - largest)
        totals = jnp.sum(exponent, axis=-1, keepdims=True)
        attn_probs = (exponent / totals).astype(jnp.bfloat16)
        attended = jnp.einsum(
            "hqk,khe->qhe", attn_probs, v_heads, preferred_element_type=jnp.float32
        )
        return (attended.reshape(row_count, D).astype(jnp.bfloat16), largest + jnp.log(totals))

    attended, log_totals = lax.map(attend, (queries, keys_all, values_all))
    branch = jnp.einsum("crd,de->cre", attended, w_out, preferred_element_type=jnp.float32) + b_out
    middle = embedded + branch
    normed2 = layer_norm(middle, ln2_gain, ln2_bias).astype(jnp.bfloat16)
    hidden_pre = (
        jnp.einsum("crd,df->crf", normed2, w_fc1, preferred_element_type=jnp.float32) + b_fc1
    )
    hidden = gelu_exact(hidden_pre).astype(jnp.bfloat16)
    output = (
        middle
        + jnp.einsum("crf,fd->crd", hidden, w_fc2, preferred_element_type=jnp.float32)
        + b_fc2
    ).astype(jnp.bfloat16)
    grad_out_f = cotangent.astype(jnp.float32)
    grad_w_fc2 = jnp.einsum("crf,crd->fd", hidden, cotangent, preferred_element_type=jnp.float32)
    grad_b_fc2 = jnp.sum(grad_out_f, axis=(0, 1))
    grad_hidden = jnp.einsum("crd,fd->crf", cotangent, w_fc2, preferred_element_type=jnp.float32)
    unused_gelu, pull_gelu = jax.vjp(gelu_exact, hidden_pre)
    grad_pre = pull_gelu(grad_hidden)[0].astype(jnp.bfloat16)
    grad_w_fc1 = jnp.einsum("crd,crf->df", normed2, grad_pre, preferred_element_type=jnp.float32)
    grad_b_fc1 = jnp.sum(grad_pre.astype(jnp.float32), axis=(0, 1))
    grad_normed2 = jnp.einsum("crf,df->crd", grad_pre, w_fc1, preferred_element_type=jnp.float32)
    unused_norm2, pull_norm2 = jax.vjp(layer_norm, middle, ln2_gain, ln2_bias)
    grad_mid_ln, grad_ln2_gain, grad_ln2_bias = pull_norm2(grad_normed2)
    grad_middle = grad_out_f + grad_mid_ln
    grad_branch = grad_middle.astype(jnp.bfloat16)
    grad_w_out = jnp.einsum(
        "crd,cre->de", attended, grad_branch, preferred_element_type=jnp.float32
    )
    grad_b_out = jnp.sum(grad_branch.astype(jnp.float32), axis=(0, 1))
    grad_attended = jnp.einsum(
        "cre,de->crd", grad_branch, w_out, preferred_element_type=jnp.float32
    ).astype(jnp.bfloat16)

    def attend_back(sliced):
        query_one, key_one, value_one, grad_one, logtot_one = sliced
        q_heads = query_one.reshape(row_count, HEADS, HEAD)
        k_heads = key_one.reshape(LEN, HEADS, HEAD)
        v_heads = value_one.reshape(LEN, HEADS, HEAD)
        g_heads = grad_one.reshape(row_count, HEADS, HEAD)
        scores = (
            jnp.einsum("qhe,khe->hqk", q_heads, k_heads, preferred_element_type=jnp.float32)
            * score_scale
        )
        attn_probs = jnp.exp(scores - logtot_one)
        grad_probs = jnp.einsum(
            "qhe,khe->hqk", g_heads, v_heads, preferred_element_type=jnp.float32
        )
        row_inner = jnp.sum(grad_probs * attn_probs, axis=-1, keepdims=True)
        grad_scores = (attn_probs * (grad_probs - row_inner)).astype(jnp.bfloat16)
        grad_query = (
            jnp.einsum(
                "hqk,khe->qhe", grad_scores, k_heads, preferred_element_type=jnp.float32
            ).reshape(row_count, D)
            * score_scale
        )
        grad_key = (
            jnp.einsum(
                "hqk,qhe->khe", grad_scores, q_heads, preferred_element_type=jnp.float32
            ).reshape(LEN, D)
            * score_scale
        )
        grad_value = jnp.einsum(
            "hqk,qhe->khe",
            attn_probs.astype(jnp.bfloat16),
            g_heads,
            preferred_element_type=jnp.float32,
        ).reshape(LEN, D)
        return (grad_query, grad_key, grad_value)

    grad_query, grad_key_part, grad_value_part = lax.map(
        attend_back, (queries, keys_all, values_all, grad_attended, log_totals)
    )
    grad_keys, grad_values = (
        lax.psum_scatter(grad_key_part, "seq", scatter_dimension=1, tiled=True),
        lax.psum_scatter(grad_value_part, "seq", scatter_dimension=1, tiled=True),
    )
    grad_qkv = jnp.concatenate(
        [
            grad_query.astype(jnp.bfloat16),
            grad_keys.astype(jnp.bfloat16),
            grad_values.astype(jnp.bfloat16),
        ],
        axis=-1,
    )
    grad_q_bias = jnp.sum(grad_qkv[..., :D].astype(jnp.float32), axis=(0, 1))
    grad_v_bias = jnp.sum(grad_qkv[..., 2 * D :].astype(jnp.float32), axis=(0, 1))
    grad_w_qkv = jnp.einsum("crd,cre->de", normed, grad_qkv, preferred_element_type=jnp.float32)
    grad_normed = jnp.einsum("cre,de->crd", grad_qkv, w_qkv, preferred_element_type=jnp.float32)
    unused_norm1, pull_norm1 = jax.vjp(layer_norm, embedded, ln1_gain, ln1_bias)
    grad_emb_ln, grad_ln1_gain, grad_ln1_bias = pull_norm1(grad_normed)
    grad_embedded = grad_middle + grad_emb_ln
    grad_mask = jnp.sum(grad_embedded * (1.0 - visible), axis=(0, 1))
    grad_proj_part = jnp.einsum("crv,crd->cvd", onehot, grad_embedded, precision=exact_prec)
    grad_projected = lax.psum(grad_proj_part.astype(jnp.bfloat16), "seq")
    grad_x = jnp.einsum("cvd,id->cvi", grad_projected, w_proj, preferred_element_type=jnp.float32)
    leading = (lax.axis_index("seq") == 0).astype(jnp.float32)
    grad_w_proj = (
        jnp.einsum("cvi,cvd->id", x_vis, grad_projected, preferred_element_type=jnp.float32)
        * leading
    )
    grad_b_proj = jnp.sum(grad_projected.astype(jnp.float32), axis=(0, 1)) * leading
    grad_list = [
        grad_w_proj,
        grad_b_proj,
        grad_mask,
        grad_ln1_gain,
        grad_ln1_bias,
        grad_w_qkv,
        grad_q_bias,
        grad_v_bias,
        grad_w_out,
        grad_b_out,
        grad_ln2_gain,
        grad_ln2_bias,
        grad_w_fc1,
        grad_b_fc1,
        grad_w_fc2,
        grad_b_fc2,
    ]
    offsets = []
    running = 0
    for tensor in grad_list:
        offsets.append(running)
        running += math.prod(tensor.shape)
    flat = jnp.concatenate([tensor.reshape(-1) for tensor in grad_list])
    matrix_slots = [0, 5, 8, 12, 14]
    matrix_list = [w_proj, w_qkv, w_out, w_fc1, w_fc2]
    counts_list = [math.prod(grad_list[slot].shape) for slot in matrix_slots]
    summed = lax.psum(flat, ("seq", "clip"))
    squares = jnp.stack(
        [
            jnp.sum(summed[offsets[slot] : offsets[slot] + counts_list[number]] ** 2)
            for number, slot in enumerate(matrix_slots)
        ]
    )
    results = [
        summed[offsets[number] : offsets[number] + math.prod(tensor.shape)].reshape(tensor.shape)
        for number, tensor in enumerate(grad_list)
    ]
    trust_all = jnp.stack(
        [
            jnp.sqrt(jnp.mean(matrix.astype(jnp.float32) ** 2))
            / jnp.sqrt(squares[number] / counts_list[number] + 1e-06)
            for number, matrix in enumerate(matrix_list)
        ]
    )
    trust = jnp.concatenate([trust_all[:1], trust_all[2:]])
    trust_qkv = trust_all[1:2]
    return (
        output,
        grad_x,
        results[0],
        results[1],
        results[2],
        results[3],
        results[4],
        results[5],
        results[6],
        results[7],
        results[8],
        results[9],
        results[10],
        results[11],
        results[12],
        results[13],
        results[14],
        results[15],
        trust,
        trust_qkv,
    )


def solution(mesh):
    return jax.shard_map(
        shards,
        mesh=mesh,
        in_specs=(
            P("clip", None, None),
            P("clip", None),
            P(),
            P(),
            P(),
            P(),
            P(),
            P(),
            P(),
            P(),
            P(),
            P(),
            P(),
            P(),
            P(),
            P(),
            P(),
            P(),
            P("clip", "seq", None),
        ),
        out_specs=(
            P("clip", "seq", None),
            P("clip", None, None),
            P(),
            P(),
            P(),
            P(),
            P(),
            P(),
            P(),
            P(),
            P(),
            P(),
            P(),
            P(),
            P(),
            P(),
            P(),
            P(),
            P(),
            P(),
        ),
        check_vma=False,
    )
```

profile of v0, /device:TPU:0, one launch (start us, length us, event | category | flops | bytes accessed | tf_op | source)
XLA Modules:
  0.0 848.6 jit_solution(2511256565757544996)
XLA Ops:
  12.2 2.8 fusion.69
  21.6 3.2 fusion.16
  26.8 28.8 %all-gather.5.cloned.1.call-done = bf16[3,1568,384]{2,1,0:T(8,128)(2,1)} async-done(((bf16[3,392,384]{2,1,0:T(8,128)(2,1)}), bf16[3,1568,384]{2,1,0:T(8,128)(2,1)}) %all-gather.5.cloned.1.call-update) | async-done | bytes 3612688 | tf_op jit(solution)/shard_map/all_gather | solution.py:75
  55.5 6.3 copy.53
  61.9 27.0 %all-gather.3.cloned.1.call-done = bf16[3,1568,384]{2,1,0:T(8,128)(2,1)} async-done(((bf16[3,392,384]{2,1,0:T(8,128)(2,1)}), bf16[3,1568,384]{2,1,0:T(8,128)(2,1)}) %all-gather.3.cloned.1.call-update) | async-done | bytes 3612688 | tf_op jit(solution)/shard_map/all_gather | solution.py:76
  88.9 6.3 copy.51
  95.2 81.8 %while.26 = (s32[]{:T(128)}, bf16[3,392,384]{1,2,0:T(8,128)(2,1)}, f32[3,6,392,1]{2,1,3,0:T(8,128)S(1)}, bf16[3,1568,384]{1,2,0:T(8,128)(2,1)}, bf16[3,392,384]{...) while((s32[]{:T(128)}, bf16[3,392,384]{1,2,0:T(8,128)(2,1)}, f32[3,6,392,1]{2,1,3,0:T(8,128)S(1)}, ...), condition=%wide.region_6.7_spmd, body=%wide.region_3.6_spmd.sunk | while | flops 977451200 | bytes 53475364 | solution.py:97
  98.3 7.9 multiply_reduce_fusion.21
  106.2 8.2 fusion.120
  114.4 7.3 fusion.121
  125.3 7.9 multiply_reduce_fusion.21
  133.2 8.2 fusion.120
  141.4 7.3 fusion.121
  152.4 7.9 multiply_reduce_fusion.21
  160.3 8.2 fusion.120
  168.5 7.3 fusion.121
  180.0 3.8 fusion.19
  183.8 17.4 %multiply_convert_fusion.1 = (bf16[3,392,1536]{2,1,0:T(8,128)(2,1)}, f32[3,392,1536]{2,1,0:T(8,128)S(1)}) fusion(f32[3,392,1536]{2,1,0:T(8,128)S(1)} %get-tuple-element.221, f32[1536]{0:T(1024)S(1)} %copy-done.55, u8[392,1536]{1,0:T(8,128)(4,1)S(1)} %get-tuple-element.140, u8[392,1536]{1,0:T(8,128)(4,1)S(1)} %get-tuple-element.139), kind=kLoop, calls=%fused_computation.39 | loop fusion | flops 128249856 | bytes 19273728 | tf_op jit(solution)/shard_map/convert_element_type | solution.py:104
  201.2 5.1 convert_reduce_fusion
  206.3 2.9 multiply_reduce_fusion.6
  214.0 159.5 %while.27 = (s32[]{:T(128)}, bf16[3,392,384]{2,1,0:T(8,128)(2,1)}, f32[3,1568,384]{2,1,0:T(8,128)}, f32[3,1568,384]{2,1,0:T(8,128)}, bf16[3,1568,384]{1,2,0:T(8,...) while((s32[]{:T(128)}, bf16[3,392,384]{2,1,0:T(8,128)(2,1)}, ...), condition=%wide.region_13.14_spmd, body=%wide.region_11.13_spmd.sunk | while | flops 2405435136 | bytes 276586112 | solution.py:167
  221.7 5.1 fusion.133
  228.0 3.2 copy.109
  231.2 14.4 %multiply_reduce_fusion.22 = (f32[6,392]{1,0:T(8,128)S(1)}, f32[6,392,1568]{2,1,0:T(8,128)}) fusion(f32[6,392,1568]{2,1,0:T(8,128)} %copy-done.1, f32[6,392]{1,0:T(8,128)S(1)} %dynamic-slice_bitcast_fusion.2, bf16[392,6,64]{0,2,1:T(8,128)(2,1)} %bitcast.165, bf16[1568,6,64]{0,2,1:T(8,128)(2,1)S(1)} %bitcast.164), kind=kOutput, calls=%fused_computation.13.clone.1 | convolution fusion | flops 486805184 | bytes 31027584 | tf_op jit(solution)/shard_map/while/body/eval_jaxpr/qhe,khe->hqk/dot_general | solution.py:142
  246.0 7.6 multiply_convert_fusion.3
  253.6 3.1 convolution_multiply_fusion.4
  262.4 4.9 constant_dynamic-update-slice_fusion.22
  274.8 5.1 fusion.133
  281.1 3.2 copy.109
  284.3 14.4 %multiply_reduce_fusion.22 = (f32[6,392]{1,0:T(8,128)S(1)}, f32[6,392,1568]{2,1,0:T(8,128)}) fusion(f32[6,392,1568]{2,1,0:T(8,128)} %copy-done.1, f32[6,392]{1,0:T(8,128)S(1)} %dynamic-slice_bitcast_fusion.2, bf16[392,6,64]{0,2,1:T(8,128)(2,1)} %bitcast.165, bf16[1568,6,64]{0,2,1:T(8,128)(2,1)S(1)} %bitcast.164), kind=kOutput, calls=%fused_computation.13.clone.1 | convolution fusion | flops 486805184 | bytes 31027584 | tf_op jit(solution)/shard_map/while/body/eval_jaxpr/qhe,khe->hqk/dot_general | solution.py:142
  299.1 7.6 multiply_convert_fusion.3
  306.6 3.1 convolution_multiply_fusion.4
  315.4 4.9 constant_dynamic-update-slice_fusion.22
  327.8 5.1 fusion.133
  334.2 3.2 copy.109
  337.3 14.4 %multiply_reduce_fusion.22 = (f32[6,392]{1,0:T(8,128)S(1)}, f32[6,392,1568]{2,1,0:T(8,128)}) fusion(f32[6,392,1568]{2,1,0:T(8,128)} %copy-done.1, f32[6,392]{1,0:T(8,128)S(1)} %dynamic-slice_bitcast_fusion.2, bf16[392,6,64]{0,2,1:T(8,128)(2,1)} %bitcast.165, bf16[1568,6,64]{0,2,1:T(8,128)(2,1)S(1)} %bitcast.164), kind=kOutput, calls=%fused_computation.13.clone.1 | convolution fusion | flops 486805184 | bytes 31027584 | tf_op jit(solution)/shard_map/while/body/eval_jaxpr/qhe,khe->hqk/dot_general | solution.py:142
  352.1 7.6 multiply_convert_fusion.3
  359.7 3.1 convolution_multiply_fusion.4
  368.5 5.0 constant_dynamic-update-slice_fusion.22
  374.8 5.7 convolution_bitcast_fusion
  380.5 4.3 reshape.293
  384.9 5.5 convolution_bitcast_fusion.1
  390.4 3.2 reshape.292
  393.6 2.8 convolution_bitcast_fusion.4
  399.9 38.5 %reduce-scatter.5.cloned.1.call-done = f32[3,392,384]{2,1,0:T(8,128)} async-done(((f32[3,1568,384]{2,1,0:T(8,128)}), f32[3,392,384]{2,1,0:T(8,128)}) %reduce-scatter.5.cloned.1.call-update) | async-done | bytes 1806352 | tf_op jit(solution)/shard_map/reduce_scatter | solution.py:172
  438.4 2.6 convert_reduce_fusion.3
  441.0 64.7 %reduce-scatter.3.cloned.1.call-done = f32[3,392,384]{2,1,0:T(8,128)} async-done(((f32[3,1568,384]{2,1,0:T(8,128)}), f32[3,392,384]{2,1,0:T(8,128)}) %reduce-scatter.3.cloned.1.call-update) | async-done | bytes 1806352 | tf_op jit(solution)/shard_map/reduce_scatter | solution.py:171
  507.4 4.0 fusion.64
  516.4 4.7 convolution_bitcast_fusion.2
  522.6 25.4 %all-reduce.3.cloned.1.call-done = bf16[3,157,384]{2,1,0:T(8,128)(2,1)} async-done(((bf16[3,157,384]{2,1,0:T(8,128)(2,1)}), bf16[3,157,384]{2,1,0:T(8,128)(2,1)}) %all-reduce.3.cloned.1.call-update) | async-done | bytes 361744 | tf_op jit(solution)/shard_map/psum | solution.py:191
  548.0 2.5 fusion.24
  550.5 2.7 copy.62
  555.5 2.5 constant_dynamic-update-slice_fusion.16
  563.3 15.5 %dynamic-update-slice.5 = f32[2069760]{0:T(1024)} dynamic-update-slice(f32[2069760]{0:T(1024)} %constant_dynamic-update-slice_fusion.12, f32[442368]{0:T(1024)S(1)} %reshape.290, s32[]{} %constant.199) | dynamic-update-slice | bytes 3538948
  587.6 21.3 %dynamic-update-slice.12 = f32[2069760]{0:T(1024)} dynamic-update-slice(f32[2069760]{0:T(1024)} %constant_dynamic-update-slice_fusion.6, f32[589824]{0:T(1024)} %reshape.292, s32[]{} %constant.206) | dynamic-update-slice | bytes 4718596
  610.2 20.1 %dynamic-update-slice.14 = f32[2069760]{0:T(1024)} dynamic-update-slice(f32[2069760]{0:T(1024)} %constant_dynamic-update-slice_fusion.5, f32[589824]{0:T(1024)S(1)} %copy-done.15, s32[]{} %constant.208) | dynamic-update-slice | bytes 4718596
  631.7 2.6 multiply_reduce_fusion.3
  635.0 2.5 multiply_reduce_fusion.5
  645.1 5.6 add_convert_fusion.1
  652.4 158.5 %all-reduce.5.cloned.1.call-done = f32[2069760]{0:T(1024)} async-done(((f32[2069760]{0:T(1024)}), f32[2069760]{0:T(1024)}) %all-reduce.5.cloned.1.call-update) | async-done | bytes 8279056 | tf_op jit(solution)/shard_map/psum | solution.py:226
  818.5 3.7 multiply_reduce_fusion.13
  822.9 5.0 multiply_reduce_fusion.4
  829.3 2.7 reshape.294
  831.9 3.4 slice.113
  (279 shorter events, 125.4 us)
Async XLA Ops:
  7.2 3.3 copy-start
  7.2 48.3 %all-gather.5.cloned.1.call-start = ((), (), s32[]{:S(2)}) async-start(), calls=%async_computation.3 | async-start | bytes 4515840 | tf_op jit(solution)/shard_map/all_gather | solution.py:75
  7.3 8.2 copy-start.49
  8.3 7.3 copy-start.40
  10.5 5.7 copy-start.23
  10.5 5.7 copy-start.53
  10.5 5.7 copy-start.61
  15.0 3.1 copy-start.6
  15.0 3.1 copy-start.34
  16.2 5.3 copy-start.58
  16.2 5.3 copy-start.59
  21.5 67.4 %all-gather.3.cloned.1.call-start = ((), (), s32[]{:S(2)}) async-start(), calls=%async_computation.2 | async-start | bytes 4515840 | tf_op jit(solution)/shard_map/all_gather | solution.py:76
  24.8 413.6 %reduce-scatter.5.cloned.1.call-start = ((), (), s32[]{:S(2)}) async-start(), calls=%async_computation.5 | async-start | bytes 9031680 | tf_op jit(solution)/shard_map/reduce_scatter | solution.py:172
  95.2 81.8 %copy-start.7 = (f32[3,392,384]{2,1,0:T(8,128)S(1)}, f32[3,392,384]{2,1,0:T(8,128)}, u32[]{:S(2)}) copy-start(f32[3,392,384]{2,1,0:T(8,128)} %copy-done.6) | copy-start | bytes 5419012
  95.2 81.8 %copy-start.25 = (bf16[384,384]{1,0:T(8,128)(2,1)S(1)}, bf16[384,384]{1,0:T(8,128)(2,1)}, u32[]{:S(2)}) copy-start(bf16[384,384]{1,0:T(8,128)(2,1)} %param.33) | copy-start | bytes 884740
  95.2 81.8 %copy-start.60 = (f32[384]{0:T(512)S(1)}, f32[384]{0:T(512)}, u32[]{:S(2)}) copy-start(f32[384]{0:T(512)} %param.34) | copy-start | bytes 4612
  179.4 29.9 %copy-start.9 = (f32[3,392,384]{2,1,0:T(8,128)}, f32[3,392,384]{2,1,0:T(8,128)S(1)}, u32[]{:S(2)}) copy-start(f32[3,392,384]{2,1,0:T(8,128)S(1)} %get-tuple-element.220) | copy-start | bytes 5419012
  179.4 29.9 %copy-start.32 = (f32[3,392]{1,0:T(4,128)}, f32[3,392]{1,0:T(4,128)S(1)}, u32[]{:S(2)}) copy-start(f32[3,392]{1,0:T(4,128)S(1)} %broadcast_multiply_fusion) | copy-start | bytes 14116
  180.0 29.3 %copy-start.36 = (f32[3,392]{1,0:T(4,128)}, f32[3,392]{1,0:T(4,128)S(1)}, u32[]{:S(2)}) copy-start(f32[3,392]{1,0:T(4,128)S(1)} %fusion.51) | copy-start | bytes 14116
  183.8 17.4 %copy-start.18 = (bf16[3,392,384]{2,1,0:T(8,128)(2,1)S(1)}, bf16[3,392,384]{2,1,0:T(8,128)(2,1)}, u32[]{:S(2)}) copy-start(bf16[3,392,384]{2,1,0:T(8,128)(2,1)} %param.41) | copy-start | bytes 2709508
  183.8 17.4 %copy-start.30 = (bf16[1536,384]{1,0:T(8,128)(2,1)S(1)}, bf16[1536,384]{1,0:T(8,128)(2,1)}, u32[]{:S(2)}) copy-start(bf16[1536,384]{1,0:T(8,128)(2,1)} %param.39) | copy-start | bytes 3538948
  210.1 3.9 copy-start.42
  214.2 3.6 copy-start.16
  221.7 6.3 copy-start.1
  231.2 14.8 %copy-start.2 = (f32[6,392,1568]{2,1,0:T(8,128)S(1)}, f32[6,392,1568]{2,1,0:T(8,128)}, u32[]{:S(2)}) copy-start(f32[6,392,1568]{2,1,0:T(8,128)} %copy-done.1) | copy-start | bytes 44255236 | tf_op jit(solution)/shard_map/while
  253.6 3.1 copy-start.4
  262.4 4.9 copy-start.17
  267.3 3.6 copy-start.16
  274.8 6.3 copy-start.1
  284.3 14.8 %copy-start.2 = (f32[6,392,1568]{2,1,0:T(8,128)S(1)}, f32[6,392,1568]{2,1,0:T(8,128)}, u32[]{:S(2)}) copy-start(f32[6,392,1568]{2,1,0:T(8,128)} %copy-done.1) | copy-start | bytes 44255236 | tf_op jit(solution)/shard_map/while
  306.6 3.1 copy-start.4
  315.4 4.9 copy-start.17
  320.3 3.6 copy-start.16
  327.8 6.3 copy-start.1
  337.3 14.8 %copy-start.2 = (f32[6,392,1568]{2,1,0:T(8,128)S(1)}, f32[6,392,1568]{2,1,0:T(8,128)}, u32[]{:S(2)}) copy-start(f32[6,392,1568]{2,1,0:T(8,128)} %copy-done.1) | copy-start | bytes 44255236 | tf_op jit(solution)/shard_map/while
  359.7 3.1 copy-start.4
  368.5 5.0 copy-start.17
  373.5 132.2 %reduce-scatter.3.cloned.1.call-start = ((), (), s32[]{:S(2)}) async-start(), calls=%async_computation.4 | async-start | bytes 9031680 | tf_op jit(solution)/shard_map/reduce_scatter | solution.py:171
  374.1 173.9 %all-reduce.3.cloned.1.call-start = ((), (), s32[]{:S(2)}) async-start(), calls=%async_computation.6 | async-start | bytes 737280 | tf_op jit(solution)/shard_map/psum | solution.py:191
  380.5 4.4 copy-start.10
  380.5 4.4 copy-start.33
  380.5 4.4 copy-start.37
  380.5 4.4 copy-start.48
  380.5 4.4 copy-start.52
  390.4 3.2 copy-start.22
  396.4 110.9 %copy-start.8 = (f32[3,392,384]{2,1,0:T(8,128)S(1)}, f32[3,392,384]{2,1,0:T(8,128)}, u32[]{:S(2)}) copy-start(f32[3,392,384]{2,1,0:T(8,128)} %copy-done.6) | copy-start | bytes 5419012
  396.4 110.9 %copy-start.35 = (f32[3,392]{1,0:T(4,128)S(1)}, f32[3,392]{1,0:T(4,128)}, u32[]{:S(2)}) copy-start(f32[3,392]{1,0:T(4,128)} %copy-done.34) | copy-start | bytes 14116
  396.4 110.9 %copy-start.54 = (f32[384]{0:T(512)S(1)}, f32[384]{0:T(512)}, u32[]{:S(2)}) copy-start(f32[384]{0:T(512)} %param.28) | copy-start | bytes 4612
  507.3 4.1 copy-start.31
  507.3 4.1 copy-start.45
  507.4 4.1 copy-start.39
  512.9 3.5 copy-start.62
  516.1 294.8 %all-reduce.5.cloned.1.call-start = ((), (), s32[]{:S(2)}) async-start(), calls=%async_computation.7 | async-start | bytes 16564224 | tf_op jit(solution)/shard_map/psum | solution.py:226
  550.5 7.5 copy-start.27
  555.5 28.2 %copy-start.56 = (f32[384]{0:T(512)S(1)}, f32[384]{0:T(512)}, u32[]{:S(2)}) copy-start(f32[384]{0:T(512)} %get-tuple-element.178) | copy-start | bytes 4612
  555.5 29.5 %copy-start.64 = (f32[384]{0:T(512)S(1)}, f32[384]{0:T(512)}, u32[]{:S(2)}) copy-start(f32[384]{0:T(512)} %get-tuple-element.143) | copy-start | bytes 4612
  555.5 30.8 %copy-start.63 = (f32[384]{0:T(512)S(1)}, f32[384]{0:T(512)}, u32[]{:S(2)}) copy-start(f32[384]{0:T(512)} %get-tuple-element.145) | copy-start | bytes 4612
  578.8 30.1 %copy-start.57 = (f32[1536]{0:T(1024)S(1)}, f32[1536]{0:T(1024)}, u32[]{:S(2)}) copy-start(f32[1536]{0:T(1024)} %get-tuple-element.224) | copy-start | bytes 18436
  578.8 31.4 %copy-start.15 = (f32[589824]{0:T(1024)S(1)}, f32[589824]{0:T(1024)}, u32[]{:S(2)}) copy-start(f32[589824]{0:T(1024)} %reshape.293) | copy-start | bytes 7077892
  631.6 9.0 %copy-start.24 = (bf16[384,1152]{1,0:T(8,128)(2,1)S(1)}, bf16[384,1152]{1,0:T(8,128)(2,1)}, u32[]{:S(2)}) copy-start(bf16[384,1152]{1,0:T(8,128)(2,1)} %param.30) | copy-start | bytes 2654212
  631.6 13.4 %copy-start.11 = (f32[3,392,384]{2,1,0:T(8,128)S(1)}, f32[3,392,384]{2,1,0:T(8,128)}, u32[]{:S(2)}) copy-start(f32[3,392,384]{2,1,0:T(8,128)} %copy-done.9) | copy-start | bytes 5419012
  631.6 13.4 %copy-start.65 = (f32[384]{0:T(512)S(1)}, f32[384]{0:T(512)}, u32[]{:S(2)}) copy-start(f32[384]{0:T(512)} %param.40) | copy-start | bytes 4612
  645.1 5.6 copy-start.26
  645.1 5.6 copy-start.28
  (22 other events, 46.2 us)
Sparse Core Ops, SparseCore 0:
  21.6 33.8 all-gather.4
  57.7 31.1 all-gather.2
  373.6 64.7 reduce-scatter.4
  441.0 64.6 reduce-scatter.2
  516.2 31.7 all-reduce.2
  631.8 179.0 all-reduce.4
where the time goes:
time: 861 us; the launch traced here: 849 us
  waiting for transfers between devices  343 us (40%)
  local copies, waits for them, and re-layouts  193 us (22%)
  matrix products  181 us (21%)
  other arithmetic  106 us (12%)
  between operations  23.5 us (3%)
    psum x1, waiting for transfers between devices, shards(): summed = lax.psum(flat, ('seq', 'clip'))  158 us
    unnamed x132, local copies, waits for them, and re-layouts  79.6 us
    reduce_scatter x1, waiting for transfers between devices, shards(): lax.psum_scatter(grad_key_part, 'seq', scatter_dimension=1, tiled=True)  64.7 us
    dot_general x3, matrix products, attend_back(): jnp.einsum('qhe,khe->hqk', g_heads, v_heads, preferred_element_type=jnp.f...  43.3 us
    reduce_scatter x1, waiting for transfers between devices, shards(): lax.psum_scatter(grad_value_part, 'seq', scatter_dimension=1, tiled=True)  38.5 us
    dynamic_update_slice x15, local copies, waits for them, and re-layouts, shards(): lax.map(attend_back, (queries, keys_all, values_all, grad_attended, log_t...  36.6 us
    all_gather x1, waiting for transfers between devices, shards(): lax.all_gather(keys_local, 'seq', axis=1, tiled=True)  28.8 us
    all_gather x1, waiting for transfers between devices, shards(): lax.all_gather(values_local, 'seq', axis=1, tiled=True)  27 us
  transfers between devices with their start and end apart: 6, of which 6 were waited for; matrix products, arithmetic and copies ran while one was open for 7% of the time, Pallas kernels for 0%

commit v1 on v0

--- a/solution.py
+++ b/solution.py
@@ -223,7 +223,7 @@
     matrix_slots = [0, 5, 8, 12, 14]
     matrix_list = [w_proj, w_qkv, w_out, w_fc1, w_fc2]
     counts_list = [math.prod(grad_list[slot].shape) for slot in matrix_slots]
-    summed = lax.psum(flat, ("seq", "clip"))
+    summed = lax.psum(lax.psum(flat, "clip"), "seq")
     squares = jnp.stack(
         [
             jnp.sum(summed[offsets[slot] : offsets[slot] + counts_list[number]] ** 2)

time: 861 us -> 1100 us (1.28)
  waiting for transfers between devices: 343 us -> 586 us
    psum x1 -> x2, waiting for transfers between devices: 158 us -> 401 us  [shards(): summed = lax.psum(lax.psum(flat, 'clip'), 'seq')]
  transfers between devices with their start and end apart: 6 -> 7, of which waited for: 6 -> 7; matrix products, arithmetic and copies ran while one was open for 7% -> 6% of each run, Pallas kernels for 0% -> 0%
where the time goes in v1:
time: 1100 us; the launch traced here: 1090 us
  waiting for transfers between devices  586 us (53%)
  local copies, waits for them, and re-layouts  193 us (18%)
  matrix products  181 us (16%)
  other arithmetic  106 us (10%)
  between operations  23.5 us (2%)
    psum x2, waiting for transfers between devices, shards(): summed = lax.psum(lax.psum(flat, 'clip'), 'seq')  401 us
    unnamed x132, local copies, waits for them, and re-layouts  79.6 us
    reduce_scatter x1, waiting for transfers between devices, shards(): lax.psum_scatter(grad_key_part, 'seq', scatter_dimension=1, tiled=True)  64.7 us
    dot_general x3, matrix products, attend_back(): jnp.einsum('qhe,khe->hqk', g_heads, v_heads, preferred_element_type=jnp.f...  43.3 us
    reduce_scatter x1, waiting for transfers between devices, shards(): lax.psum_scatter(grad_value_part, 'seq', scatter_dimension=1, tiled=True)  38.5 us
    dynamic_update_slice x15, local copies, waits for them, and re-layouts, shards(): lax.map(attend_back, (queries, keys_all, values_all, grad_attended, log_t...  36.6 us
    all_gather x1, waiting for transfers between devices, shards(): lax.all_gather(keys_local, 'seq', axis=1, tiled=True)  28.8 us
    all_gather x1, waiting for transfers between devices, shards(): lax.all_gather(values_local, 'seq', axis=1, tiled=True)  27 us
  transfers between devices with their start and end apart: 7, of which 7 were waited for; matrix products, arithmetic and copies ran while one was open for 6% of the time, Pallas kernels for 0%

profile of v1, /device:TPU:0, one launch (start us, length us, event | category | flops | bytes accessed | tf_op | source)
XLA Modules:
  0.0 1091.5 jit_solution(6682455427097610238)
XLA Ops:
  12.2 2.8 fusion.69
  21.6 3.2 fusion.16
  26.8 28.8 %all-gather.5.cloned.1.call-done = bf16[3,1568,384]{2,1,0:T(8,128)(2,1)} async-done(((bf16[3,392,384]{2,1,0:T(8,128)(2,1)}), bf16[3,1568,384]{2,1,0:T(8,128)(2,1)}) %all-gather.5.cloned.1.call-update) | async-done | bytes 3612688 | tf_op jit(solution)/shard_map/all_gather | solution.py:75
  55.5 6.3 copy.53
  61.9 27.0 %all-gather.3.cloned.1.call-done = bf16[3,1568,384]{2,1,0:T(8,128)(2,1)} async-done(((bf16[3,392,384]{2,1,0:T(8,128)(2,1)}), bf16[3,1568,384]{2,1,0:T(8,128)(2,1)}) %all-gather.3.cloned.1.call-update) | async-done | bytes 3612688 | tf_op jit(solution)/shard_map/all_gather | solution.py:76
  88.9 6.3 copy.51
  95.2 81.8 %while.26 = (s32[]{:T(128)}, bf16[3,392,384]{1,2,0:T(8,128)(2,1)}, f32[3,6,392,1]{2,1,3,0:T(8,128)S(1)}, bf16[3,1568,384]{1,2,0:T(8,128)(2,1)}, bf16[3,392,384]{...) while((s32[]{:T(128)}, bf16[3,392,384]{1,2,0:T(8,128)(2,1)}, f32[3,6,392,1]{2,1,3,0:T(8,128)S(1)}, ...), condition=%wide.region_6.7_spmd, body=%wide.region_3.6_spmd.sunk | while | flops 977451200 | bytes 53475364 | solution.py:97
  98.3 7.9 multiply_reduce_fusion.21
  106.2 8.2 fusion.120
  114.4 7.3 fusion.121
  125.3 7.9 multiply_reduce_fusion.21
  133.2 8.2 fusion.120
  141.4 7.3 fusion.121
  152.4 7.9 multiply_reduce_fusion.21
  160.3 8.2 fusion.120
  168.5 7.3 fusion.121
  180.0 3.8 fusion.19
  183.8 17.4 %multiply_convert_fusion.1 = (bf16[3,392,1536]{2,1,0:T(8,128)(2,1)}, f32[3,392,1536]{2,1,0:T(8,128)S(1)}) fusion(f32[3,392,1536]{2,1,0:T(8,128)S(1)} %get-tuple-element.221, f32[1536]{0:T(1024)S(1)} %copy-done.55, u8[392,1536]{1,0:T(8,128)(4,1)S(1)} %get-tuple-element.140, u8[392,1536]{1,0:T(8,128)(4,1)S(1)} %get-tuple-element.139), kind=kLoop, calls=%fused_computation.39 | loop fusion | flops 128249856 | bytes 19273728 | tf_op jit(solution)/shard_map/convert_element_type | solution.py:104
  201.2 5.1 convert_reduce_fusion
  206.3 2.9 multiply_reduce_fusion.6
  214.0 159.5 %while.27 = (s32[]{:T(128)}, bf16[3,392,384]{2,1,0:T(8,128)(2,1)}, f32[3,1568,384]{2,1,0:T(8,128)}, f32[3,1568,384]{2,1,0:T(8,128)}, bf16[3,1568,384]{1,2,0:T(8,...) while((s32[]{:T(128)}, bf16[3,392,384]{2,1,0:T(8,128)(2,1)}, ...), condition=%wide.region_13.14_spmd, body=%wide.region_11.13_spmd.sunk | while | flops 2405435136 | bytes 276586112 | solution.py:167
  221.7 5.1 fusion.133
  228.0 3.2 copy.109
  231.2 14.4 %multiply_reduce_fusion.22 = (f32[6,392]{1,0:T(8,128)S(1)}, f32[6,392,1568]{2,1,0:T(8,128)}) fusion(f32[6,392,1568]{2,1,0:T(8,128)} %copy-done.1, f32[6,392]{1,0:T(8,128)S(1)} %dynamic-slice_bitcast_fusion.2, bf16[392,6,64]{0,2,1:T(8,128)(2,1)} %bitcast.165, bf16[1568,6,64]{0,2,1:T(8,128)(2,1)S(1)} %bitcast.164), kind=kOutput, calls=%fused_computation.13.clone.1 | convolution fusion | flops 486805184 | bytes 31027584 | tf_op jit(solution)/shard_map/while/body/eval_jaxpr/qhe,khe->hqk/dot_general | solution.py:142
  246.0 7.6 multiply_convert_fusion.3
  253.6 3.1 convolution_multiply_fusion.4
  262.4 4.9 constant_dynamic-update-slice_fusion.22
  274.8 5.1 fusion.133
  281.1 3.2 copy.109
  284.3 14.4 %multiply_reduce_fusion.22 = (f32[6,392]{1,0:T(8,128)S(1)}, f32[6,392,1568]{2,1,0:T(8,128)}) fusion(f32[6,392,1568]{2,1,0:T(8,128)} %copy-done.1, f32[6,392]{1,0:T(8,128)S(1)} %dynamic-slice_bitcast_fusion.2, bf16[392,6,64]{0,2,1:T(8,128)(2,1)} %bitcast.165, bf16[1568,6,64]{0,2,1:T(8,128)(2,1)S(1)} %bitcast.164), kind=kOutput, calls=%fused_computation.13.clone.1 | convolution fusion | flops 486805184 | bytes 31027584 | tf_op jit(solution)/shard_map/while/body/eval_jaxpr/qhe,khe->hqk/dot_general | solution.py:142
  299.1 7.6 multiply_convert_fusion.3
  306.6 3.1 convolution_multiply_fusion.4
  315.4 4.9 constant_dynamic-update-slice_fusion.22
  327.8 5.1 fusion.133
  334.2 3.2 copy.109
  337.3 14.4 %multiply_reduce_fusion.22 = (f32[6,392]{1,0:T(8,128)S(1)}, f32[6,392,1568]{2,1,0:T(8,128)}) fusion(f32[6,392,1568]{2,1,0:T(8,128)} %copy-done.1, f32[6,392]{1,0:T(8,128)S(1)} %dynamic-slice_bitcast_fusion.2, bf16[392,6,64]{0,2,1:T(8,128)(2,1)} %bitcast.165, bf16[1568,6,64]{0,2,1:T(8,128)(2,1)S(1)} %bitcast.164), kind=kOutput, calls=%fused_computation.13.clone.1 | convolution fusion | flops 486805184 | bytes 31027584 | tf_op jit(solution)/shard_map/while/body/eval_jaxpr/qhe,khe->hqk/dot_general | solution.py:142
  352.1 7.6 multiply_convert_fusion.3
  359.7 3.1 convolution_multiply_fusion.4
  368.5 5.0 constant_dynamic-update-slice_fusion.22
  374.8 5.7 convolution_bitcast_fusion
  380.5 4.3 reshape.293
  384.9 5.5 convolution_bitcast_fusion.1
  390.4 3.2 reshape.292
  393.6 2.8 convolution_bitcast_fusion.4
  399.9 38.5 %reduce-scatter.5.cloned.1.call-done = f32[3,392,384]{2,1,0:T(8,128)} async-done(((f32[3,1568,384]{2,1,0:T(8,128)}), f32[3,392,384]{2,1,0:T(8,128)}) %reduce-scatter.5.cloned.1.call-update) | async-done | bytes 1806352 | tf_op jit(solution)/shard_map/reduce_scatter | solution.py:172
  438.4 2.6 convert_reduce_fusion.3
  441.0 64.7 %reduce-scatter.3.cloned.1.call-done = f32[3,392,384]{2,1,0:T(8,128)} async-done(((f32[3,1568,384]{2,1,0:T(8,128)}), f32[3,392,384]{2,1,0:T(8,128)}) %reduce-scatter.3.cloned.1.call-update) | async-done | bytes 1806352 | tf_op jit(solution)/shard_map/reduce_scatter | solution.py:171
  507.4 4.0 fusion.64
  516.2 4.7 convolution_bitcast_fusion.2
  522.4 25.6 %all-reduce.4.cloned.1.call-done = bf16[3,157,384]{2,1,0:T(8,128)(2,1)} async-done(((bf16[3,157,384]{2,1,0:T(8,128)(2,1)}), bf16[3,157,384]{2,1,0:T(8,128)(2,1)}) %all-reduce.4.cloned.1.call-update) | async-done | bytes 361744 | tf_op jit(solution)/shard_map/psum | solution.py:191
  548.0 2.5 fusion.24
  550.5 2.7 copy.62
  555.5 2.5 constant_dynamic-update-slice_fusion.16
  563.3 15.5 %dynamic-update-slice.5 = f32[2069760]{0:T(1024)} dynamic-update-slice(f32[2069760]{0:T(1024)} %constant_dynamic-update-slice_fusion.12, f32[442368]{0:T(1024)S(1)} %reshape.290, s32[]{} %constant.199) | dynamic-update-slice | bytes 3538948
  587.6 21.3 %dynamic-update-slice.12 = f32[2069760]{0:T(1024)} dynamic-update-slice(f32[2069760]{0:T(1024)} %constant_dynamic-update-slice_fusion.6, f32[589824]{0:T(1024)} %reshape.292, s32[]{} %constant.206) | dynamic-update-slice | bytes 4718596
  610.2 20.1 %dynamic-update-slice.14 = f32[2069760]{0:T(1024)} dynamic-update-slice(f32[2069760]{0:T(1024)} %constant_dynamic-update-slice_fusion.5, f32[589824]{0:T(1024)S(1)} %copy-done.15, s32[]{} %constant.208) | dynamic-update-slice | bytes 4718596
  631.9 268.5 %all-reduce.6.cloned.1.call-done = f32[2069760]{0:T(1024)} async-done(((f32[2069760]{0:T(1024)}), f32[2069760]{0:T(1024)}) %all-reduce.6.cloned.1.call-update) | async-done | bytes 8279056 | tf_op jit(solution)/shard_map/psum | solution.py:226
  900.4 2.6 multiply_reduce_fusion.3
  913.9 5.4 add_convert_fusion.1
  921.0 132.7 %all-reduce.8.cloned.1.call-done = f32[2069760]{0:T(1024)} async-done(((f32[2069760]{0:T(1024)}), f32[2069760]{0:T(1024)}) %all-reduce.8.cloned.1.call-update) | async-done | bytes 8279056 | tf_op jit(solution)/shard_map/psum | solution.py:226
  1061.4 3.7 multiply_reduce_fusion.13
  1065.8 5.0 multiply_reduce_fusion.4
  1072.1 2.7 reshape.294
  1074.8 3.4 slice.113
  (282 shorter events, 128.1 us)
Async XLA Ops:
  7.2 3.3 copy-start
  7.2 48.3 %all-gather.5.cloned.1.call-start = ((), (), s32[]{:S(2)}) async-start(), calls=%async_computation.3 | async-start | bytes 4515840 | tf_op jit(solution)/shard_map/all_gather | solution.py:75
  7.3 8.2 copy-start.49
  8.3 7.3 copy-start.40
  10.5 5.7 copy-start.23
  10.5 5.7 copy-start.53
  10.5 5.7 copy-start.61
  15.0 3.1 copy-start.6
  16.2 5.3 copy-start.58
  16.2 5.3 copy-start.59
  21.5 67.4 %all-gather.3.cloned.1.call-start = ((), (), s32[]{:S(2)}) async-start(), calls=%async_computation.2 | async-start | bytes 4515840 | tf_op jit(solution)/shard_map/all_gather | solution.py:76
  24.8 413.6 %reduce-scatter.5.cloned.1.call-start = ((), (), s32[]{:S(2)}) async-start(), calls=%async_computation.5 | async-start | bytes 9031680 | tf_op jit(solution)/shard_map/reduce_scatter | solution.py:172
  95.2 81.8 %copy-start.7 = (f32[3,392,384]{2,1,0:T(8,128)S(1)}, f32[3,392,384]{2,1,0:T(8,128)}, u32[]{:S(2)}) copy-start(f32[3,392,384]{2,1,0:T(8,128)} %copy-done.6) | copy-start | bytes 5419012
  95.2 81.8 %copy-start.25 = (bf16[384,384]{1,0:T(8,128)(2,1)S(1)}, bf16[384,384]{1,0:T(8,128)(2,1)}, u32[]{:S(2)}) copy-start(bf16[384,384]{1,0:T(8,128)(2,1)} %param.33) | copy-start | bytes 884740
  95.2 81.8 %copy-start.60 = (f32[384]{0:T(512)S(1)}, f32[384]{0:T(512)}, u32[]{:S(2)}) copy-start(f32[384]{0:T(512)} %param.34) | copy-start | bytes 4612
  179.4 29.9 %copy-start.9 = (f32[3,392,384]{2,1,0:T(8,128)}, f32[3,392,384]{2,1,0:T(8,128)S(1)}, u32[]{:S(2)}) copy-start(f32[3,392,384]{2,1,0:T(8,128)S(1)} %get-tuple-element.220) | copy-start | bytes 5419012
  179.4 29.9 %copy-start.32 = (f32[3,392]{1,0:T(4,128)}, f32[3,392]{1,0:T(4,128)S(1)}, u32[]{:S(2)}) copy-start(f32[3,392]{1,0:T(4,128)S(1)} %broadcast_multiply_fusion) | copy-start | bytes 14116
  180.0 29.3 %copy-start.36 = (f32[3,392]{1,0:T(4,128)}, f32[3,392]{1,0:T(4,128)S(1)}, u32[]{:S(2)}) copy-start(f32[3,392]{1,0:T(4,128)S(1)} %fusion.51) | copy-start | bytes 14116
  183.8 17.4 %copy-start.18 = (bf16[3,392,384]{2,1,0:T(8,128)(2,1)S(1)}, bf16[3,392,384]{2,1,0:T(8,128)(2,1)}, u32[]{:S(2)}) copy-start(bf16[3,392,384]{2,1,0:T(8,128)(2,1)} %param.41) | copy-start | bytes 2709508
  183.8 17.4 %copy-start.30 = (bf16[1536,384]{1,0:T(8,128)(2,1)S(1)}, bf16[1536,384]{1,0:T(8,128)(2,1)}, u32[]{:S(2)}) copy-start(bf16[1536,384]{1,0:T(8,128)(2,1)} %param.39) | copy-start | bytes 3538948
  210.1 3.9 copy-start.42
  214.2 3.6 copy-start.16
  221.7 6.3 copy-start.1
  231.2 14.8 %copy-start.2 = (f32[6,392,1568]{2,1,0:T(8,128)S(1)}, f32[6,392,1568]{2,1,0:T(8,128)}, u32[]{:S(2)}) copy-start(f32[6,392,1568]{2,1,0:T(8,128)} %copy-done.1) | copy-start | bytes 44255236 | tf_op jit(solution)/shard_map/while
  253.6 3.1 copy-start.4
  262.4 4.9 copy-start.17
  267.3 3.6 copy-start.16
  274.8 6.3 copy-start.1
  284.3 14.8 %copy-start.2 = (f32[6,392,1568]{2,1,0:T(8,128)S(1)}, f32[6,392,1568]{2,1,0:T(8,128)}, u32[]{:S(2)}) copy-start(f32[6,392,1568]{2,1,0:T(8,128)} %copy-done.1) | copy-start | bytes 44255236 | tf_op jit(solution)/shard_map/while
  306.6 3.1 copy-start.4
  315.4 4.9 copy-start.17
  320.3 3.6 copy-start.16
  327.8 6.3 copy-start.1
  337.3 14.8 %copy-start.2 = (f32[6,392,1568]{2,1,0:T(8,128)S(1)}, f32[6,392,1568]{2,1,0:T(8,128)}, u32[]{:S(2)}) copy-start(f32[6,392,1568]{2,1,0:T(8,128)} %copy-done.1) | copy-start | bytes 44255236 | tf_op jit(solution)/shard_map/while
  359.7 3.1 copy-start.4
  368.5 5.0 copy-start.17
  373.5 132.2 %reduce-scatter.3.cloned.1.call-start = ((), (), s32[]{:S(2)}) async-start(), calls=%async_computation.4 | async-start | bytes 9031680 | tf_op jit(solution)/shard_map/reduce_scatter | solution.py:171
  374.1 173.9 %all-reduce.4.cloned.1.call-start = ((), (), s32[]{:S(2)}) async-start(), calls=%async_computation.6 | async-start | bytes 737280 | tf_op jit(solution)/shard_map/psum | solution.py:191
  380.5 4.4 copy-start.10
  380.5 4.4 copy-start.33
  380.5 4.4 copy-start.37
  380.5 4.4 copy-start.48
  380.5 4.4 copy-start.52
  390.4 3.2 copy-start.22
  396.4 110.9 %copy-start.8 = (f32[3,392,384]{2,1,0:T(8,128)S(1)}, f32[3,392,384]{2,1,0:T(8,128)}, u32[]{:S(2)}) copy-start(f32[3,392,384]{2,1,0:T(8,128)} %copy-done.6) | copy-start | bytes 5419012
  396.4 110.9 %copy-start.35 = (f32[3,392]{1,0:T(4,128)S(1)}, f32[3,392]{1,0:T(4,128)}, u32[]{:S(2)}) copy-start(f32[3,392]{1,0:T(4,128)} %copy-done.34) | copy-start | bytes 14116
  396.4 110.9 %copy-start.54 = (f32[384]{0:T(512)S(1)}, f32[384]{0:T(512)}, u32[]{:S(2)}) copy-start(f32[384]{0:T(512)} %param.28) | copy-start | bytes 4612
  507.3 4.1 copy-start.31
  507.3 4.1 copy-start.45
  507.4 4.1 copy-start.39
  512.9 3.3 copy-start.62
  516.1 384.3 %all-reduce.6.cloned.1.call-start = ((), (), s32[]{:S(2)}) async-start(), calls=%async_computation.7 | async-start | bytes 16564224 | tf_op jit(solution)/shard_map/psum | solution.py:226
  550.5 7.5 copy-start.27
  555.5 28.2 %copy-start.56 = (f32[384]{0:T(512)S(1)}, f32[384]{0:T(512)}, u32[]{:S(2)}) copy-start(f32[384]{0:T(512)} %get-tuple-element.178) | copy-start | bytes 4612
  555.5 29.5 %copy-start.64 = (f32[384]{0:T(512)S(1)}, f32[384]{0:T(512)}, u32[]{:S(2)}) copy-start(f32[384]{0:T(512)} %get-tuple-element.143) | copy-start | bytes 4612
  555.5 30.8 %copy-start.63 = (f32[384]{0:T(512)S(1)}, f32[384]{0:T(512)}, u32[]{:S(2)}) copy-start(f32[384]{0:T(512)} %get-tuple-element.145) | copy-start | bytes 4612
  578.8 30.1 %copy-start.57 = (f32[1536]{0:T(1024)S(1)}, f32[1536]{0:T(1024)}, u32[]{:S(2)}) copy-start(f32[1536]{0:T(1024)} %get-tuple-element.224) | copy-start | bytes 18436
  578.8 31.4 %copy-start.15 = (f32[589824]{0:T(1024)S(1)}, f32[589824]{0:T(1024)}, u32[]{:S(2)}) copy-start(f32[589824]{0:T(1024)} %reshape.293) | copy-start | bytes 7077892
  631.6 422.2 %all-reduce.8.cloned.1.call-start = ((), (), s32[]{:S(2)}) async-start(), calls=%async_computation.8 | async-start | bytes 16564224 | tf_op jit(solution)/shard_map/psum | solution.py:226
  900.4 9.1 copy-start.24
  900.4 13.5 %copy-start.11 = (f32[3,392,384]{2,1,0:T(8,128)S(1)}, f32[3,392,384]{2,1,0:T(8,128)}, u32[]{:S(2)}) copy-start(f32[3,392,384]{2,1,0:T(8,128)} %copy-done.9) | copy-start | bytes 5419012
  900.4 13.5 %copy-start.65 = (f32[384]{0:T(512)S(1)}, f32[384]{0:T(512)}, u32[]{:S(2)}) copy-start(f32[384]{0:T(512)} %param.40) | copy-start | bytes 4612
  913.9 5.4 copy-start.26
  913.9 5.4 copy-start.28
  (23 other events, 49.3 us)
Sparse Core Ops, SparseCore 0:
  21.6 33.8 all-gather.4
  57.7 31.1 all-gather.2
  373.6 64.7 reduce-scatter.4
  441.0 64.6 reduce-scatter.2
  516.2 31.7 all-reduce.3
  631.7 268.6 all-reduce.5
  903.1 150.6 all-reduce.7
